TPU v7x, 32 devices: a whole 2x2x4 slice. The times are simulated.
32 devices in a mesh: tm: 4 (over z), gx: 2 (over y), gy: 4 (over x, core).
Axes of the slice: x: 2, y: 2, z: 4, core: 2. Of those that a mesh axis runs over, the one named last changes fastest.
Arguments:
- segment_opening_values: float32 [4, 4, 24, 64, 128], P('tm', None, 'gx', 'gy'), may hold values from -6 to 6
- cell_material_label: int32 [24, 64, 128], P('gx', 'gy'), may hold values from 0 to 5
- material_rigidity: float32 [6], replicated, may hold values from 0.3 to 3
- dilation_mismatch: float32 [6], replicated, may hold values from -1 to 1
- heat_swings_array: float32 [4, 2], P('tm'), may hold values from 0.5 to 4
- prony_coefficients: float32 [3], replicated, may hold values from 0.2 to 2
- prony_decay_times: float32 [3], replicated, may hold values from 0.7 to 48
Outputs:
- end_state: float32 [4, 4, 24, 64, 128], P('tm', None, 'gx', 'gy')
All inputs are finite; a program needn't handle non-finite values.
Results may differ from a plain program's by a relative error of at most 0.0001.
Values sent between devices are 32-bit elements; how exact they have to be, the bound alone decides.
A program may use at most 64 MiB of HBM per device.

v0:
```python
import jax
import jax.numpy as jnp
from jax import lax
from jax.sharding import PartitionSpec as P

PARTITION_PACES = 2
SHARP_SOLVER_ITER = 3
LOOSE_SOLVER_ITER = 2


corners = [
    (near_one, near_two, near_three)
    for near_one in (0, 1)
    for near_two in (0, 1)
    for near_three in (0, 1)
]
diagonal_weights = [1.0 / 3.0] * 8
thermal_weights = [0.25 * (2 * near_three - 1) for near_one, near_two, near_three in corners]


def from_behind(value, axis, steps):
    count = lax.axis_size(axis)
    initial, last = (max(0, -steps), min(count, count - steps))
    return lax.ppermute(value, axis, [(source, source + steps) for source in range(initial, last)])


def padded_2(block, sides, width):
    for axis, dim in sides:
        count = lax.axis_size(axis)
        forward = [(i, i + 1) for i in range(count - 1)]
        backward = [(target, source) for source, target in forward]
        low = lax.ppermute(
            lax.slice_in_dim(block, block.shape[dim] - width, None, axis=dim), axis, forward
        )
        high = lax.ppermute(lax.slice_in_dim(block, 0, width, axis=dim), axis, backward)
        block = jnp.concatenate([low, block, high], axis=dim)
    return block


def region_lookup(cell_material_label, region_table):
    looked_up = jnp.zeros(cell_material_label.shape, region_table.dtype)
    for region in range(region_table.shape[0]):
        looked_up = looked_up + jnp.where(
            cell_material_label == region, region_table[region], jnp.zeros((), region_table.dtype)
        )
    return looked_up


def stencil_apply(padded, cell_rigidity):
    extent_one, extent_two, extent_three = cell_rigidity.shape
    values = [
        padded[
            near_one : near_one + extent_one,
            near_two : near_two + extent_two,
            near_three : near_three + extent_three,
        ]
        for near_one, near_two, near_three in corners
    ]
    corner_total = values[0]
    for corner_value in values[1:]:
        corner_total = corner_total + corner_value
    result = None
    for corner_index, (near_one, near_two, near_three) in enumerate(corners):
        face_sum = values[corner_index ^ 4] + values[corner_index ^ 2] + values[corner_index ^ 1]
        element_part = cell_rigidity * (
            5.0 / 12.0 * values[corner_index] + (face_sum - corner_total) / 12.0
        )
        node_part = element_part[
            1 - near_one : extent_one - near_one,
            1 - near_two : extent_two - near_two,
            1 - near_three : extent_three - near_three,
        ]
        result = node_part if result is None else result + node_part
    return result


def nodal_sum(element_field, weights):
    extent_one, extent_two, extent_three = element_field.shape
    result = None
    for corner_index, (near_one, near_two, near_three) in enumerate(corners):
        node_part = (
            weights[corner_index]
            * element_field[
                1 - near_one : extent_one - near_one,
                1 - near_two : extent_two - near_two,
                1 - near_three : extent_three - near_three,
            ]
        )
        result = node_part if result is None else result + node_part
    return result


def on_device(
    segment_opening_values,
    cell_material_label,
    material_rigidity,
    dilation_mismatch,
    heat_swings_array,
    prony_coefficients,
    prony_decay_times,
):
    extent_one, extent_two, extent_three = cell_material_label.shape
    margin = 1
    depth_rim = margin - 1
    grid_one = extent_one * lax.axis_size("gx")
    grid_two = extent_two * lax.axis_size("gy")
    anchor_one = lax.axis_index("gx") * extent_one
    anchor_two = lax.axis_index("gy") * extent_two
    lower_row = from_behind(cell_material_label[-1:], "gx", 1)
    taller = jnp.concatenate([lower_row, cell_material_label], axis=0)
    lower_column = from_behind(taller[:, -1:], "gy", 1)
    ids_wide = jnp.concatenate([lower_column, taller], axis=1)
    element_one = anchor_one - margin + lax.iota(jnp.int32, extent_one + 2 * margin - 1)
    element_two = anchor_two - margin + lax.iota(jnp.int32, extent_two + 2 * margin - 1)
    element_inside = ((element_one >= 0) & (element_one < grid_one))[:, None, None] & (
        (element_two >= 0) & (element_two < grid_two)
    )[None, :, None]
    coefficient = jnp.where(
        element_inside,
        region_lookup(ids_wide, material_rigidity),
        jnp.zeros((), material_rigidity.dtype),
    )
    loaded = coefficient * region_lookup(ids_wide, dilation_mismatch)
    cell_rigidity = jnp.pad(coefficient, ((0, 0), (0, 0), (1, 0)))
    element_load = jnp.pad(loaded, ((0, 0), (0, 0), (1, 0)))
    thermal_wide = nodal_sum(element_load, thermal_weights)
    rigidity_main_terms = nodal_sum(cell_rigidity, diagonal_weights)
    node_one = anchor_one - depth_rim + lax.iota(jnp.int32, extent_one + 2 * depth_rim)
    node_two = anchor_two - depth_rim + lax.iota(jnp.int32, extent_two + 2 * depth_rim)
    node_inside = ((node_one >= 0) & (node_one < grid_one))[:, None, None] & (
        (node_two >= 0) & (node_two < grid_two)
    )[None, :, None]

    def inner_sum(left, right):
        return jnp.sum(left * right)

    def apply_operator(field, shift_value):
        padded = jnp.pad(padded_2(field, (("gx", 0), ("gy", 1)), 1), ((0, 0), (0, 0), (1, 1)))
        return shift_value * field + stencil_apply(padded, cell_rigidity)

    def pair_sum(remainder, scaled, image):
        return lax.psum((inner_sum(remainder, scaled), inner_sum(image, scaled)), ("gx", "gy"))

    def conjugate_solve(rhs_field, initial, shift_value, iterations):
        diagonal = shift_value + rigidity_main_terms
        solution = initial
        remainder = rhs_field - apply_operator(solution, shift_value)
        scaled = jnp.where(node_inside, remainder / diagonal, 0.0)
        image = apply_operator(scaled, shift_value)
        gamma_now, curvature_sum = pair_sum(remainder, scaled, image)
        step_size = gamma_now / curvature_sum
        search = scaled
        along = image
        blend = 0.0
        for iteration in range(iterations):
            if iteration > 0:
                search = scaled + blend * search
                along = image + blend * along
            solution = solution + step_size * search
            if iteration + 1 < iterations:
                remainder = remainder - step_size * along
                scaled = jnp.where(node_inside, remainder / diagonal, 0.0)
                image = apply_operator(scaled, shift_value)
                gamma_next, curvature_sum = pair_sum(remainder, scaled, image)
                blend = gamma_next / gamma_now
                step_size = gamma_next / (curvature_sum - blend * gamma_next / step_size)
                gamma_now = gamma_next
        return solution

    def moment_forward(present_displacements, heat_level, step_length, iterations):
        decay_rate = jnp.exp(-step_length / prony_decay_times)
        factors = prony_coefficients * decay_rate
        shift_value = 1.0 / step_length + jnp.sum(factors)
        history = present_displacements[1:]
        rhs_field = (
            present_displacements[0] / step_length
            + heat_level * thermal_wide
            + jnp.sum(factors[:, None, None, None] * history, axis=0)
        )
        displaced = conjugate_solve(rhs_field, present_displacements[0], shift_value, iterations)
        history = (
            decay_rate[:, None, None, None] * history
            + (1.0 - decay_rate)[:, None, None, None] * displaced[None]
        )
        return jnp.concatenate([displaced[None], history], axis=0)

    segment_number = lax.axis_index("tm")
    launch_moment = segment_opening_values[0]
    heat_trajectory = heat_swings_array[0]
    loose_interval_span = 1.0 * PARTITION_PACES
    sharp_result = launch_moment
    for sharp_interval_span in range(PARTITION_PACES):
        sharp_result = moment_forward(
            sharp_result, heat_trajectory[sharp_interval_span], 1.0, SHARP_SOLVER_ITER
        )
    coarse_old = moment_forward(
        launch_moment, heat_trajectory[PARTITION_PACES - 1], loose_interval_span, LOOSE_SOLVER_ITER
    )
    correction = sharp_result - coarse_old
    finished = coarse_old + correction

    def next_turn(turn_index, carried):
        received = from_behind(carried, "tm", 1)
        ongoing_approx = jnp.where(segment_number == 0, launch_moment, received)
        return (
            moment_forward(
                ongoing_approx,
                heat_trajectory[PARTITION_PACES - 1],
                loose_interval_span,
                LOOSE_SOLVER_ITER,
            )
            + correction
        )

    finished = lax.fori_loop(0, lax.axis_size("tm") - 1, next_turn, finished)
    return finished[None]


def solution(mesh):
    placed = (
        P("tm", None, "gx", "gy", None),
        P("gx", "gy", None),
        P(),
        P(),
        P("tm", None),
        P(),
        P(),
    )
    return jax.shard_map(
        on_device,
        mesh=mesh,
        in_specs=placed,
        out_specs=P("tm", None, "gx", "gy", None),
        check_vma=False,
    )
```

profile of v0, /device:TPU:25, one launch (start us, length us, event | category | flops | bytes accessed | tf_op | source)
XLA Modules:
  0.0 552.9 jit_solution(6058032627438427017)
XLA Ops:
  14.6 4.0 collective-permute-start.14
  22.9 7.5 %add_select_fusion = (f32[13,17,128]{2,1,0:T(8,128)S(1)}, f32[13,17,128]{2,1,0:T(8,128)S(1)}) fusion(f32[]{:T(128)} %bitcast.7, f32[]{:T(128)} %bitcast.6, f32[]{:T(128)} %bitcast.5, f32[]{:T(128)} %bitcast.4, f32[]{:T(128)} %bitcast.3, f32[]{:T(128)} %bitcast.2, pred[13,17]{1,0:T(8,128)(4,1)S(1)} %broadcast_and_fusion.1, ...), kind=kLoop, calls=%fused_computation.304 | loop fusion | flops 876928 | bytes 339725 | tf_op jit(solution)/shard_map/jit(_where)/select_n | solution.py:118
  33.7 4.3 collective-permute-start.27
  42.4 4.6 collective-permute-start.29
  54.1 10.1 %all-reduce.22 = (f32[]{:T(128)}, f32[]{:T(128)}) all-reduce(f32[]{:T(128)} %get-tuple-element.198, f32[]{:T(128)} %get-tuple-element.197), channel_id=1, replica_groups=mesh['tm'=4,'gx'=2,'gy'=4] {'gx','gy'}, use_global_device_ids=true, to_apply=%region_13.14 | all-reduce | flops 2 | bytes 16 | tf_op jit(solution)/shard_map/psum | solution.py:142
  72.6 4.4 collective-permute-start.33
  84.2 10.1 %all-reduce.21 = (f32[]{:T(128)}, f32[]{:T(128)}) all-reduce(f32[]{:T(128)} %get-tuple-element.196, f32[]{:T(128)} %get-tuple-element.195), channel_id=1, replica_groups=mesh['tm'=4,'gx'=2,'gy'=4] {'gx','gy'}, use_global_device_ids=true, to_apply=%region_17.18 | all-reduce | flops 2 | bytes 16 | tf_op jit(solution)/shard_map/psum | solution.py:142
  106.4 4.4 collective-permute-start.37
  117.9 10.1 %all-reduce.20 = (f32[]{:T(128)}, f32[]{:T(128)}) all-reduce(f32[]{:T(128)} %get-tuple-element.271, f32[]{:T(128)} %fusion.269), channel_id=1, replica_groups=mesh['tm'=4,'gx'=2,'gy'=4] {'gx','gy'}, use_global_device_ids=true, to_apply=%region_21.22 | all-reduce | flops 2 | bytes 16 | tf_op jit(solution)/shard_map/psum | solution.py:142
  139.0 4.4 collective-permute-start.41
  156.3 3.4 collective-permute-start.45
  166.8 10.3 %all-reduce.19 = (f32[]{:T(128)}, f32[]{:T(128)}) all-reduce(f32[]{:T(128)} %get-tuple-element.194, f32[]{:T(128)} %get-tuple-element.193), channel_id=1, replica_groups=mesh['tm'=4,'gx'=2,'gy'=4] {'gx','gy'}, use_global_device_ids=true, to_apply=%region_26.27 | all-reduce | flops 2 | bytes 16 | tf_op jit(solution)/shard_map/psum | solution.py:142
  183.1 4.0 collective-permute-start.19
  188.5 3.8 collective-permute-start.49
  194.3 3.6 collective-permute-start.21
  206.3 11.8 %all-reduce.18 = (f32[]{:T(128)}, f32[]{:T(128)}, f32[]{:T(128)}, f32[]{:T(128)}) all-reduce(f32[]{:T(128)} %get-tuple-element.200, f32[]{:T(128)} %get-tuple-element.199, f32[]{:T(128)} %get-tuple-element.192, f32[]{:T(128)} %get-tuple-element.191), channel_id=1, replica_groups=mesh['tm'=4,'gx'=2,'gy'=4] {'gx','gy'}, use_global_device_ids=true, to_apply=%region_3.4 | all-reduce | flops 4 | bytes 32 | tf_op jit(solution)/shard_map/psum | solution.py:142
  228.4 4.0 collective-permute-start.23
  233.8 5.0 collective-permute-start.53
  240.8 3.6 collective-permute-start.25
  252.8 12.0 %all-reduce.17 = (f32[]{:T(128)}, f32[]{:T(128)}, f32[]{:T(128)}, f32[]{:T(128)}) all-reduce(f32[]{:T(128)} %get-tuple-element.501, f32[]{:T(128)} %fusion.367, f32[]{:T(128)} %get-tuple-element.258, f32[]{:T(128)} %fusion.138), channel_id=1, replica_groups=mesh['tm'=4,'gx'=2,'gy'=4] {'gx','gy'}, use_global_device_ids=true, to_apply=%region_7.8 | all-reduce | flops 4 | bytes 32 | tf_op jit(solution)/shard_map/psum | solution.py:142
  273.3 278.8 %while.13 = (s32[]{:T(128)}, f32[4,12,16,128]{3,2,1,0:T(8,128)S(1)}, pred[]{:T(512)}, f32[4,12,16,128]{3,2,1,0:T(8,128)S(1)}, f32[2]{0:T(128)S(1)}, /*index=5*/f...) while((s32[]{:T(128)}, ...), condition=%wide.region_48.49_spmd.clone, body=%wide.region_37.48_spmd.clone.sunk | while | flops 7646898 | bytes 29306644 | solution.py:215
  276.5 7.7 %collective-permute-done = f32[4,12,16,128]{3,2,1,0:T(8,128)S(1)} collective-permute-done((f32[4,12,16,128]{3,2,1,0:T(8,128)S(1)}, f32[4,12,16,128]{3,2,1,0:T(8,128)S(1)}, u32[]{:S(2)}, u32[]{:S(2)}) %collective-permute-start) | collective-permute-done | bytes 393248 | tf_op jit(solution)/shard_map/while/body/eval_jaxpr/ppermute | solution.py:24
  285.6 4.0 collective-permute-start.2
  290.3 5.6 %collective-permute-start.3 = (f32[14,1,128]{2,1,0:T(1,128)S(1)}, f32[14,1,128]{2,1,0:T(1,128)S(1)}, u32[]{:S(2)}, u32[]{:S(2)}) collective-permute-start(f32[14,1,128]{2,1,0:T(1,128)S(1)} %get-tuple-element.691), channel_id=1, source_target_pairs={{1,0},{2,1},{3,2},{5,4},{6,5},{7,6},{9,8},{10,9},{11,10},{13,12},{... | collective-permute-start | bytes 21512 | tf_op jit(solution)/shard_map/while/body/eval_jaxpr/ppermute | solution.py:35
  296.0 3.2 collective-permute-start.4
  303.5 4.0 collective-permute-start.6
  310.6 5.0 collective-permute-start.8
  318.6 13.7 %all-reduce.25 = (f32[]{:T(128)}, f32[]{:T(128)}) all-reduce(f32[]{:T(128)} %get-tuple-element.727, f32[]{:T(128)} %get-tuple-element.728), channel_id=1, replica_groups=mesh['tm'=4,'gx'=2,'gy'=4] {'gx','gy'}, use_global_device_ids=true, to_apply=%region_41.41 | all-reduce | flops 2 | bytes 16 | tf_op jit(solution)/shard_map/while/body/eval_jaxpr/psum | solution.py:142
  340.3 5.0 collective-permute-start.11
  350.6 12.0 %all-reduce.26 = (f32[]{:T(128)}, f32[]{:T(128)}) all-reduce(f32[]{:T(128)} %get-tuple-element.732, f32[]{:T(128)} %fusion.532), channel_id=1, replica_groups=mesh['tm'=4,'gx'=2,'gy'=4] {'gx','gy'}, use_global_device_ids=true, to_apply=%region_45.45 | all-reduce | flops 2 | bytes 16 | tf_op jit(solution)/shard_map/while/body/eval_jaxpr/psum | solution.py:142
  370.2 8.4 %collective-permute-done = f32[4,12,16,128]{3,2,1,0:T(8,128)S(1)} collective-permute-done((f32[4,12,16,128]{3,2,1,0:T(8,128)S(1)}, f32[4,12,16,128]{3,2,1,0:T(8,128)S(1)}, u32[]{:S(2)}, u32[]{:S(2)}) %collective-permute-start) | collective-permute-done | bytes 393248 | tf_op jit(solution)/shard_map/while/body/eval_jaxpr/ppermute | solution.py:24
  380.0 4.0 collective-permute-start.2
  384.7 4.9 collective-permute-start.3
  396.3 4.0 collective-permute-start.6
  401.0 3.2 collective-permute-start.7
  404.3 3.9 collective-permute-start.8
  411.2 13.7 %all-reduce.25 = (f32[]{:T(128)}, f32[]{:T(128)}) all-reduce(f32[]{:T(128)} %get-tuple-element.727, f32[]{:T(128)} %get-tuple-element.728), channel_id=1, replica_groups=mesh['tm'=4,'gx'=2,'gy'=4] {'gx','gy'}, use_global_device_ids=true, to_apply=%region_41.41 | all-reduce | flops 2 | bytes 16 | tf_op jit(solution)/shard_map/while/body/eval_jaxpr/psum | solution.py:142
  432.9 5.0 collective-permute-start.11
  443.2 12.0 %all-reduce.26 = (f32[]{:T(128)}, f32[]{:T(128)}) all-reduce(f32[]{:T(128)} %get-tuple-element.732, f32[]{:T(128)} %fusion.532), channel_id=1, replica_groups=mesh['tm'=4,'gx'=2,'gy'=4] {'gx','gy'}, use_global_device_ids=true, to_apply=%region_45.45 | all-reduce | flops 2 | bytes 16 | tf_op jit(solution)/shard_map/while/body/eval_jaxpr/psum | solution.py:142
  462.8 8.4 %collective-permute-done = f32[4,12,16,128]{3,2,1,0:T(8,128)S(1)} collective-permute-done((f32[4,12,16,128]{3,2,1,0:T(8,128)S(1)}, f32[4,12,16,128]{3,2,1,0:T(8,128)S(1)}, u32[]{:S(2)}, u32[]{:S(2)}) %collective-permute-start) | collective-permute-done | bytes 393248 | tf_op jit(solution)/shard_map/while/body/eval_jaxpr/ppermute | solution.py:24
  472.5 4.0 collective-permute-start.2
  477.3 4.9 collective-permute-start.3
  488.9 4.0 collective-permute-start.6
  493.6 3.2 collective-permute-start.7
  496.8 3.9 collective-permute-start.8
  503.8 13.7 %all-reduce.25 = (f32[]{:T(128)}, f32[]{:T(128)}) all-reduce(f32[]{:T(128)} %get-tuple-element.727, f32[]{:T(128)} %get-tuple-element.728), channel_id=1, replica_groups=mesh['tm'=4,'gx'=2,'gy'=4] {'gx','gy'}, use_global_device_ids=true, to_apply=%region_41.41 | all-reduce | flops 2 | bytes 16 | tf_op jit(solution)/shard_map/while/body/eval_jaxpr/psum | solution.py:142
  525.4 5.0 collective-permute-start.11
  535.8 12.0 %all-reduce.26 = (f32[]{:T(128)}, f32[]{:T(128)}) all-reduce(f32[]{:T(128)} %get-tuple-element.732, f32[]{:T(128)} %fusion.532), channel_id=1, replica_groups=mesh['tm'=4,'gx'=2,'gy'=4] {'gx','gy'}, use_global_device_ids=true, to_apply=%region_45.45 | all-reduce | flops 2 | bytes 16 | tf_op jit(solution)/shard_map/while/body/eval_jaxpr/psum | solution.py:142
  (318 shorter events, 203.5 us)
Async XLA Ops:
  0.7 13.8 %collective-permute-start.13 = (s32[1,16,128]{2,1,0:T(8,128)S(1)}, s32[1,16,128]{2,1,0:T(8,128)S(1)}, u32[]{:S(2)}, u32[]{:S(2)}) collective-permute-start(s32[1,16,128]{2,1,0:T(8,128)S(1)} %slice.1138), channel_id=1, source_target_pairs={{0,4},{1,5},{2,6},{3,7},{8,12},{9,13},{10,14},{11,15},{16,20},{17,... | collective-permute-start | bytes 24584 | tf_op jit(solution)/shard_map/ppermute | solution.py:24
  4.6 14.0 %collective-permute-start.15 = (f32[1,16,128]{2,1,0:T(8,128)S(1)}, f32[1,16,128]{2,1,0:T(8,128)S(1)}, u32[]{:S(2)}, u32[]{:S(2)}) collective-permute-start(f32[1,16,128]{2,1,0:T(8,128)S(1)} %get-tuple-element.347), channel_id=1, source_target_pairs={{0,4},{1,5},{2,6},{3,7},{8,12},{9,13},{10,14},{11,15},{16,20},{17,... | collective-permute-start | bytes 24584 | tf_op jit(solution)/shard_map/ppermute | solution.py:32
  5.8 12.7 %collective-permute-start.16 = (f32[1,16,128]{2,1,0:T(8,128)S(1)}, f32[1,16,128]{2,1,0:T(8,128)S(1)}, u32[]{:S(2)}, u32[]{:S(2)}) collective-permute-start(f32[1,16,128]{2,1,0:T(8,128)S(1)} %get-tuple-element.348), channel_id=1, source_target_pairs={{4,0},{5,1},{6,2},{7,3},{12,8},{13,9},{14,10},{15,11},{20,16},{21,... | collective-permute-start | bytes 24584 | tf_op jit(solution)/shard_map/ppermute | solution.py:35
  14.6 8.4 %collective-permute-start.14 = (s32[13,1,128]{2,1,0:T(1,128)S(1)}, s32[13,1,128]{2,1,0:T(1,128)S(1)}, u32[]{:S(2)}, u32[]{:S(2)}) collective-permute-start(s32[13,1,128]{2,1,0:T(1,128)S(1)} %slice.1590), channel_id=1, source_target_pairs={{0,1},{1,2},{2,3},{4,5},{5,6},{6,7},{8,9},{9,10},{10,11},{12,13},{... | collective-permute-start | bytes 19976 | tf_op jit(solution)/shard_map/ppermute | solution.py:24
  18.6 11.9 %collective-permute-start.17 = (f32[14,1,128]{2,1,0:T(1,128)S(1)}, f32[14,1,128]{2,1,0:T(1,128)S(1)}, u32[]{:S(2)}, u32[]{:S(2)}) collective-permute-start(f32[14,1,128]{2,1,0:T(1,128)S(1)} %get-tuple-element.499), channel_id=1, source_target_pairs={{0,1},{1,2},{2,3},{4,5},{5,6},{6,7},{8,9},{9,10},{10,11},{12,13},{... | collective-permute-start | bytes 21512 | tf_op jit(solution)/shard_map/ppermute | solution.py:32
  20.5 10.0 %collective-permute-start.18 = (f32[14,1,128]{2,1,0:T(1,128)S(1)}, f32[14,1,128]{2,1,0:T(1,128)S(1)}, u32[]{:S(2)}, u32[]{:S(2)}) collective-permute-start(f32[14,1,128]{2,1,0:T(1,128)S(1)} %get-tuple-element.500), channel_id=1, source_target_pairs={{1,0},{2,1},{3,2},{5,4},{6,5},{7,6},{9,8},{10,9},{11,10},{13,12},{... | collective-permute-start | bytes 21512 | tf_op jit(solution)/shard_map/ppermute | solution.py:35
  33.7 5.6 %collective-permute-start.27 = (f32[1,16,128]{2,1,0:T(8,128)S(1)}, f32[1,16,128]{2,1,0:T(8,128)S(1)}, u32[]{:S(2)}, u32[]{:S(2)}) collective-permute-start(f32[1,16,128]{2,1,0:T(8,128)S(1)} %get-tuple-element.520), channel_id=1, source_target_pairs={{0,4},{1,5},{2,6},{3,7},{8,12},{9,13},{10,14},{11,15},{16,20},{17,... | collective-permute-start | bytes 24584 | tf_op jit(solution)/shard_map/ppermute | solution.py:32
  42.4 6.5 %collective-permute-start.29 = (f32[14,1,128]{2,1,0:T(1,128)S(1)}, f32[14,1,128]{2,1,0:T(1,128)S(1)}, u32[]{:S(2)}, u32[]{:S(2)}) collective-permute-start(f32[14,1,128]{2,1,0:T(1,128)S(1)} %get-tuple-element.497), channel_id=1, source_target_pairs={{0,1},{1,2},{2,3},{4,5},{5,6},{6,7},{8,9},{9,10},{10,11},{12,13},{... | collective-permute-start | bytes 21512 | tf_op jit(solution)/shard_map/ppermute | solution.py:32
  47.0 5.0 collective-permute-start.30
  72.6 6.4 %collective-permute-start.33 = (f32[14,1,128]{2,1,0:T(1,128)S(1)}, f32[14,1,128]{2,1,0:T(1,128)S(1)}, u32[]{:S(2)}, u32[]{:S(2)}) collective-permute-start(f32[14,1,128]{2,1,0:T(1,128)S(1)} %get-tuple-element.495), channel_id=1, source_target_pairs={{0,1},{1,2},{2,3},{4,5},{5,6},{6,7},{8,9},{9,10},{10,11},{12,13},{... | collective-permute-start | bytes 21512 | tf_op jit(solution)/shard_map/ppermute | solution.py:32
  106.4 6.4 %collective-permute-start.37 = (f32[14,1,128]{2,1,0:T(1,128)S(1)}, f32[14,1,128]{2,1,0:T(1,128)S(1)}, u32[]{:S(2)}, u32[]{:S(2)}) collective-permute-start(f32[14,1,128]{2,1,0:T(1,128)S(1)} %get-tuple-element.493), channel_id=1, source_target_pairs={{0,1},{1,2},{2,3},{4,5},{5,6},{6,7},{8,9},{9,10},{10,11},{12,13},{... | collective-permute-start | bytes 21512 | tf_op jit(solution)/shard_map/ppermute | solution.py:32
  110.8 5.0 collective-permute-start.38
  139.0 6.5 %collective-permute-start.41 = (f32[14,1,128]{2,1,0:T(1,128)S(1)}, f32[14,1,128]{2,1,0:T(1,128)S(1)}, u32[]{:S(2)}, u32[]{:S(2)}) collective-permute-start(f32[14,1,128]{2,1,0:T(1,128)S(1)} %get-tuple-element.489), channel_id=1, source_target_pairs={{0,1},{1,2},{2,3},{4,5},{5,6},{6,7},{8,9},{9,10},{10,11},{12,13},{... | collective-permute-start | bytes 21512 | tf_op jit(solution)/shard_map/ppermute | solution.py:32
  143.4 5.0 collective-permute-start.42
  156.3 6.1 %collective-permute-start.45 = (f32[14,1,128]{2,1,0:T(1,128)S(1)}, f32[14,1,128]{2,1,0:T(1,128)S(1)}, u32[]{:S(2)}, u32[]{:S(2)}) collective-permute-start(f32[14,1,128]{2,1,0:T(1,128)S(1)} %get-tuple-element.487), channel_id=1, source_target_pairs={{0,1},{1,2},{2,3},{4,5},{5,6},{6,7},{8,9},{9,10},{10,11},{12,13},{... | collective-permute-start | bytes 21512 | tf_op jit(solution)/shard_map/ppermute | solution.py:32
  179.1 9.3 %collective-permute-start.47 = (f32[1,16,128]{2,1,0:T(8,128)S(1)}, f32[1,16,128]{2,1,0:T(8,128)S(1)}, u32[]{:S(2)}, u32[]{:S(2)}) collective-permute-start(f32[1,16,128]{2,1,0:T(8,128)S(1)} %get-tuple-element.508), channel_id=1, source_target_pairs={{0,4},{1,5},{2,6},{3,7},{8,12},{9,13},{10,14},{11,15},{16,20},{17,... | collective-permute-start | bytes 24584 | tf_op jit(solution)/shard_map/ppermute | solution.py:32
  181.8 6.6 %collective-permute-start.48 = (f32[1,16,128]{2,1,0:T(8,128)S(1)}, f32[1,16,128]{2,1,0:T(8,128)S(1)}, u32[]{:S(2)}, u32[]{:S(2)}) collective-permute-start(f32[1,16,128]{2,1,0:T(8,128)S(1)} %get-tuple-element.509), channel_id=1, source_target_pairs={{4,0},{5,1},{6,2},{7,3},{12,8},{13,9},{14,10},{15,11},{20,16},{21,... | collective-permute-start | bytes 24584 | tf_op jit(solution)/shard_map/ppermute | solution.py:35
  183.1 11.1 %collective-permute-start.19 = (f32[1,16,128]{2,1,0:T(8,128)S(1)}, f32[1,16,128]{2,1,0:T(8,128)S(1)}, u32[]{:S(2)}, u32[]{:S(2)}) collective-permute-start(f32[1,16,128]{2,1,0:T(8,128)S(1)} %get-tuple-element.514), channel_id=1, source_target_pairs={{0,4},{1,5},{2,6},{3,7},{8,12},{9,13},{10,14},{11,15},{16,20},{17,... | collective-permute-start | bytes 24584 | tf_op jit(solution)/shard_map/ppermute | solution.py:32
  187.1 7.1 %collective-permute-start.20 = (f32[1,16,128]{2,1,0:T(8,128)S(1)}, f32[1,16,128]{2,1,0:T(8,128)S(1)}, u32[]{:S(2)}, u32[]{:S(2)}) collective-permute-start(f32[1,16,128]{2,1,0:T(8,128)S(1)} %get-tuple-element.515), channel_id=1, source_target_pairs={{4,0},{5,1},{6,2},{7,3},{12,8},{13,9},{14,10},{15,11},{20,16},{21,... | collective-permute-start | bytes 24584 | tf_op jit(solution)/shard_map/ppermute | solution.py:35
  188.5 11.4 %collective-permute-start.49 = (f32[14,1,128]{2,1,0:T(1,128)S(1)}, f32[14,1,128]{2,1,0:T(1,128)S(1)}, u32[]{:S(2)}, u32[]{:S(2)}) collective-permute-start(f32[14,1,128]{2,1,0:T(1,128)S(1)} %get-tuple-element.485), channel_id=1, source_target_pairs={{0,1},{1,2},{2,3},{4,5},{5,6},{6,7},{8,9},{9,10},{10,11},{12,13},{... | collective-permute-start | bytes 21512 | tf_op jit(solution)/shard_map/ppermute | solution.py:32
  192.3 7.6 %collective-permute-start.50 = (f32[14,1,128]{2,1,0:T(1,128)S(1)}, f32[14,1,128]{2,1,0:T(1,128)S(1)}, u32[]{:S(2)}, u32[]{:S(2)}) collective-permute-start(f32[14,1,128]{2,1,0:T(1,128)S(1)} %get-tuple-element.486), channel_id=1, source_target_pairs={{1,0},{2,1},{3,2},{5,4},{6,5},{7,6},{9,8},{10,9},{11,10},{13,12},{... | collective-permute-start | bytes 21512 | tf_op jit(solution)/shard_map/ppermute | solution.py:35
  194.3 6.5 %collective-permute-start.21 = (f32[14,1,128]{2,1,0:T(1,128)S(1)}, f32[14,1,128]{2,1,0:T(1,128)S(1)}, u32[]{:S(2)}, u32[]{:S(2)}) collective-permute-start(f32[14,1,128]{2,1,0:T(1,128)S(1)} %get-tuple-element.491), channel_id=1, source_target_pairs={{0,1},{1,2},{2,3},{4,5},{5,6},{6,7},{8,9},{9,10},{10,11},{12,13},{... | collective-permute-start | bytes 21512 | tf_op jit(solution)/shard_map/ppermute | solution.py:32
  224.6 9.2 %collective-permute-start.51 = (f32[1,16,128]{2,1,0:T(8,128)S(1)}, f32[1,16,128]{2,1,0:T(8,128)S(1)}, u32[]{:S(2)}, u32[]{:S(2)}) collective-permute-start(f32[1,16,128]{2,1,0:T(8,128)S(1)} %get-tuple-element.504), channel_id=1, source_target_pairs={{0,4},{1,5},{2,6},{3,7},{8,12},{9,13},{10,14},{11,15},{16,20},{17,... | collective-permute-start | bytes 24584 | tf_op jit(solution)/shard_map/ppermute | solution.py:32
  227.1 6.6 %collective-permute-start.52 = (f32[1,16,128]{2,1,0:T(8,128)S(1)}, f32[1,16,128]{2,1,0:T(8,128)S(1)}, u32[]{:S(2)}, u32[]{:S(2)}) collective-permute-start(f32[1,16,128]{2,1,0:T(8,128)S(1)} %get-tuple-element.505), channel_id=1, source_target_pairs={{4,0},{5,1},{6,2},{7,3},{12,8},{13,9},{14,10},{15,11},{20,16},{21,... | collective-permute-start | bytes 24584 | tf_op jit(solution)/shard_map/ppermute | solution.py:35
  228.4 12.3 %collective-permute-start.23 = (f32[1,16,128]{2,1,0:T(8,128)S(1)}, f32[1,16,128]{2,1,0:T(8,128)S(1)}, u32[]{:S(2)}, u32[]{:S(2)}) collective-permute-start(f32[1,16,128]{2,1,0:T(8,128)S(1)} %get-tuple-element.506), channel_id=1, source_target_pairs={{0,4},{1,5},{2,6},{3,7},{8,12},{9,13},{10,14},{11,15},{16,20},{17,... | collective-permute-start | bytes 24584 | tf_op jit(solution)/shard_map/ppermute | solution.py:32
  232.4 8.3 %collective-permute-start.24 = (f32[1,16,128]{2,1,0:T(8,128)S(1)}, f32[1,16,128]{2,1,0:T(8,128)S(1)}, u32[]{:S(2)}, u32[]{:S(2)}) collective-permute-start(f32[1,16,128]{2,1,0:T(8,128)S(1)} %get-tuple-element.507), channel_id=1, source_target_pairs={{4,0},{5,1},{6,2},{7,3},{12,8},{13,9},{14,10},{15,11},{20,16},{21,... | collective-permute-start | bytes 24584 | tf_op jit(solution)/shard_map/ppermute | solution.py:35
  233.8 12.6 %collective-permute-start.53 = (f32[14,1,128]{2,1,0:T(1,128)S(1)}, f32[14,1,128]{2,1,0:T(1,128)S(1)}, u32[]{:S(2)}, u32[]{:S(2)}) collective-permute-start(f32[14,1,128]{2,1,0:T(1,128)S(1)} %get-tuple-element.481), channel_id=1, source_target_pairs={{0,1},{1,2},{2,3},{4,5},{5,6},{6,7},{8,9},{9,10},{10,11},{12,13},{... | collective-permute-start | bytes 21512 | tf_op jit(solution)/shard_map/ppermute | solution.py:32
  238.8 7.6 %collective-permute-start.54 = (f32[14,1,128]{2,1,0:T(1,128)S(1)}, f32[14,1,128]{2,1,0:T(1,128)S(1)}, u32[]{:S(2)}, u32[]{:S(2)}) collective-permute-start(f32[14,1,128]{2,1,0:T(1,128)S(1)} %get-tuple-element.482), channel_id=1, source_target_pairs={{1,0},{2,1},{3,2},{5,4},{6,5},{7,6},{9,8},{10,9},{11,10},{13,12},{... | collective-permute-start | bytes 21512 | tf_op jit(solution)/shard_map/ppermute | solution.py:35
  240.8 6.6 %collective-permute-start.25 = (f32[14,1,128]{2,1,0:T(1,128)S(1)}, f32[14,1,128]{2,1,0:T(1,128)S(1)}, u32[]{:S(2)}, u32[]{:S(2)}) collective-permute-start(f32[14,1,128]{2,1,0:T(1,128)S(1)} %get-tuple-element.483), channel_id=1, source_target_pairs={{0,1},{1,2},{2,3},{4,5},{5,6},{6,7},{8,9},{9,10},{10,11},{12,13},{... | collective-permute-start | bytes 21512 | tf_op jit(solution)/shard_map/ppermute | solution.py:32
  273.3 10.9 %collective-permute-start = (f32[4,12,16,128]{3,2,1,0:T(8,128)S(1)}, f32[4,12,16,128]{3,2,1,0:T(8,128)S(1)}, u32[]{:S(2)}, u32[]{:S(2)}) collective-permute-start(f32[4,12,16,128]{3,2,1,0:T(8,128)S(1)} %get-tuple-element.769), channel_id=1, source_target_pairs={{0,8},{8,16},{16,24},{1,9},{9,17},{17,25},{2,10},{10,18},{18,26},{... | collective-permute-start | bytes 1179656 | tf_op jit(solution)/shard_map/while/body/eval_jaxpr/ppermute | solution.py:24
  284.3 5.3 collective-permute-start.1
  290.3 8.9 %collective-permute-start.3 = (f32[14,1,128]{2,1,0:T(1,128)S(1)}, f32[14,1,128]{2,1,0:T(1,128)S(1)}, u32[]{:S(2)}, u32[]{:S(2)}) collective-permute-start(f32[14,1,128]{2,1,0:T(1,128)S(1)} %get-tuple-element.691), channel_id=1, source_target_pairs={{1,0},{2,1},{3,2},{5,4},{6,5},{7,6},{9,8},{10,9},{11,10},{13,12},{... | collective-permute-start | bytes 21512 | tf_op jit(solution)/shard_map/while/body/eval_jaxpr/ppermute | solution.py:35
  302.2 5.3 collective-permute-start.5
  308.3 7.3 %collective-permute-start.7 = (f32[14,1,128]{2,1,0:T(1,128)S(1)}, f32[14,1,128]{2,1,0:T(1,128)S(1)}, u32[]{:S(2)}, u32[]{:S(2)}) collective-permute-start(f32[14,1,128]{2,1,0:T(1,128)S(1)} %get-tuple-element.711), channel_id=1, source_target_pairs={{1,0},{2,1},{3,2},{5,4},{6,5},{7,6},{9,8},{10,9},{11,10},{13,12},{... | collective-permute-start | bytes 21512 | tf_op jit(solution)/shard_map/while/body/eval_jaxpr/ppermute | solution.py:35
  310.6 5.7 %collective-permute-start.8 = (f32[14,1,128]{2,1,0:T(1,128)S(1)}, f32[14,1,128]{2,1,0:T(1,128)S(1)}, u32[]{:S(2)}, u32[]{:S(2)}) collective-permute-start(f32[14,1,128]{2,1,0:T(1,128)S(1)} %get-tuple-element.712), channel_id=1, source_target_pairs={{0,1},{1,2},{2,3},{4,5},{5,6},{6,7},{8,9},{9,10},{10,11},{12,13},{... | collective-permute-start | bytes 21512 | tf_op jit(solution)/shard_map/while/body/eval_jaxpr/ppermute | solution.py:32
  340.3 7.2 %collective-permute-start.11 = (f32[14,1,128]{2,1,0:T(1,128)S(1)}, f32[14,1,128]{2,1,0:T(1,128)S(1)}, u32[]{:S(2)}, u32[]{:S(2)}) collective-permute-start(f32[14,1,128]{2,1,0:T(1,128)S(1)} %get-tuple-element.735), channel_id=1, source_target_pairs={{1,0},{2,1},{3,2},{5,4},{6,5},{7,6},{9,8},{10,9},{11,10},{13,12},{... | collective-permute-start | bytes 21512 | tf_op jit(solution)/shard_map/while/body/eval_jaxpr/ppermute | solution.py:35
  367.0 11.6 %collective-permute-start = (f32[4,12,16,128]{3,2,1,0:T(8,128)S(1)}, f32[4,12,16,128]{3,2,1,0:T(8,128)S(1)}, u32[]{:S(2)}, u32[]{:S(2)}) collective-permute-start(f32[4,12,16,128]{3,2,1,0:T(8,128)S(1)} %get-tuple-element.769), channel_id=1, source_target_pairs={{0,8},{8,16},{16,24},{1,9},{9,17},{17,25},{2,10},{10,18},{18,26},{... | collective-permute-start | bytes 1179656 | tf_op jit(solution)/shard_map/while/body/eval_jaxpr/ppermute | solution.py:24
  378.7 5.3 collective-permute-start.1
  384.7 7.1 %collective-permute-start.3 = (f32[14,1,128]{2,1,0:T(1,128)S(1)}, f32[14,1,128]{2,1,0:T(1,128)S(1)}, u32[]{:S(2)}, u32[]{:S(2)}) collective-permute-start(f32[14,1,128]{2,1,0:T(1,128)S(1)} %get-tuple-element.691), channel_id=1, source_target_pairs={{1,0},{2,1},{3,2},{5,4},{6,5},{7,6},{9,8},{10,9},{11,10},{13,12},{... | collective-permute-start | bytes 21512 | tf_op jit(solution)/shard_map/while/body/eval_jaxpr/ppermute | solution.py:35
  395.0 5.3 collective-permute-start.5
  401.0 7.1 %collective-permute-start.7 = (f32[14,1,128]{2,1,0:T(1,128)S(1)}, f32[14,1,128]{2,1,0:T(1,128)S(1)}, u32[]{:S(2)}, u32[]{:S(2)}) collective-permute-start(f32[14,1,128]{2,1,0:T(1,128)S(1)} %get-tuple-element.711), channel_id=1, source_target_pairs={{1,0},{2,1},{3,2},{5,4},{6,5},{7,6},{9,8},{10,9},{11,10},{13,12},{... | collective-permute-start | bytes 21512 | tf_op jit(solution)/shard_map/while/body/eval_jaxpr/ppermute | solution.py:35
  432.9 7.2 %collective-permute-start.11 = (f32[14,1,128]{2,1,0:T(1,128)S(1)}, f32[14,1,128]{2,1,0:T(1,128)S(1)}, u32[]{:S(2)}, u32[]{:S(2)}) collective-permute-start(f32[14,1,128]{2,1,0:T(1,128)S(1)} %get-tuple-element.735), channel_id=1, source_target_pairs={{1,0},{2,1},{3,2},{5,4},{6,5},{7,6},{9,8},{10,9},{11,10},{13,12},{... | collective-permute-start | bytes 21512 | tf_op jit(solution)/shard_map/while/body/eval_jaxpr/ppermute | solution.py:35
  459.6 11.6 %collective-permute-start = (f32[4,12,16,128]{3,2,1,0:T(8,128)S(1)}, f32[4,12,16,128]{3,2,1,0:T(8,128)S(1)}, u32[]{:S(2)}, u32[]{:S(2)}) collective-permute-start(f32[4,12,16,128]{3,2,1,0:T(8,128)S(1)} %get-tuple-element.769), channel_id=1, source_target_pairs={{0,8},{8,16},{16,24},{1,9},{9,17},{17,25},{2,10},{10,18},{18,26},{... | collective-permute-start | bytes 1179656 | tf_op jit(solution)/shard_map/while/body/eval_jaxpr/ppermute | solution.py:24
  471.2 5.3 collective-permute-start.1
  477.3 7.1 %collective-permute-start.3 = (f32[14,1,128]{2,1,0:T(1,128)S(1)}, f32[14,1,128]{2,1,0:T(1,128)S(1)}, u32[]{:S(2)}, u32[]{:S(2)}) collective-permute-start(f32[14,1,128]{2,1,0:T(1,128)S(1)} %get-tuple-element.691), channel_id=1, source_target_pairs={{1,0},{2,1},{3,2},{5,4},{6,5},{7,6},{9,8},{10,9},{11,10},{13,12},{... | collective-permute-start | bytes 21512 | tf_op jit(solution)/shard_map/while/body/eval_jaxpr/ppermute | solution.py:35
  487.6 5.3 collective-permute-start.5
  493.6 7.1 %collective-permute-start.7 = (f32[14,1,128]{2,1,0:T(1,128)S(1)}, f32[14,1,128]{2,1,0:T(1,128)S(1)}, u32[]{:S(2)}, u32[]{:S(2)}) collective-permute-start(f32[14,1,128]{2,1,0:T(1,128)S(1)} %get-tuple-element.711), channel_id=1, source_target_pairs={{1,0},{2,1},{3,2},{5,4},{6,5},{7,6},{9,8},{10,9},{11,10},{13,12},{... | collective-permute-start | bytes 21512 | tf_op jit(solution)/shard_map/while/body/eval_jaxpr/ppermute | solution.py:35
  525.4 7.2 %collective-permute-start.11 = (f32[14,1,128]{2,1,0:T(1,128)S(1)}, f32[14,1,128]{2,1,0:T(1,128)S(1)}, u32[]{:S(2)}, u32[]{:S(2)}) collective-permute-start(f32[14,1,128]{2,1,0:T(1,128)S(1)} %get-tuple-element.735), channel_id=1, source_target_pairs={{1,0},{2,1},{3,2},{5,4},{6,5},{7,6},{9,8},{10,9},{11,10},{13,12},{... | collective-permute-start | bytes 21512 | tf_op jit(solution)/shard_map/while/body/eval_jaxpr/ppermute | solution.py:35
  (41 other events, 143.7 us)
where the time goes:
time: 557 us; the launch traced here: 553 us
  starting transfers between devices  217 us (39%)
  blocking collectives  141 us (25%)
  waiting for transfers between devices  79.3 us (14%)
  other arithmetic  54.4 us (10%)
  between operations  26.8 us (5%)
  loops' own time  19.1 us (3%)
  local copies, waits for them, and re-layouts  14.9 us (3%)
    psum x12, blocking collectives, pair_sum(): lax.psum((inner_sum(remainder, scaled), inner_sum(image, scaled)), ('gx',...  141 us
    ppermute x38, starting transfers between devices, padded_2(): lax.ppermute(lax.slice_in_dim(block, block.shape[dim] - width, None, axis...  123 us
    ppermute x38, starting transfers between devices, padded_2(): lax.ppermute(lax.slice_in_dim(block, 0, width, axis=dim), axis, backward)  83.2 us
    ppermute x38, waiting for transfers between devices, padded_2(): lax.ppermute(lax.slice_in_dim(block, 0, width, axis=dim), axis, backward)  43.1 us
    ppermute x5, waiting for transfers between devices, from_behind(): lax.ppermute(value, axis, [(source, source + steps) for source in range(i...  24.5 us
    reduce_sum x19, other arithmetic, inner_sum(): return jnp.sum(left * right)  21.7 us
    another operation x1, loops' own time, on_device(): finished = lax.fori_loop(0, lax.axis_size('tm') - 1, next_turn, finished)  19.1 us
    ppermute x38, waiting for transfers between devices, padded_2(): lax.ppermute(lax.slice_in_dim(block, block.shape[dim] - width, None, axis...  11.6 us
  transfers between devices with their start and end apart: 81, of which 33 were waited for; matrix products, arithmetic and copies ran while one was open for 4% of the time, Pallas kernels for 0%

commit v1 on v0

v1 whole, which is shorter than its diff:
```python
import functools

import jax
import jax.numpy as jnp
from jax import lax
from jax.experimental import pallas as pl
from jax.experimental.pallas import tpu as pltpu
from jax.sharding import PartitionSpec as P

PARTITION_PACES = 2
SHARP_SOLVER_ITER = 3
LOOSE_SOLVER_ITER = 2
MESH = pl.DeviceIdType.MESH
F32 = jnp.float32
PAD = 8
UNROLL = 2

LAB, U0, H1, HC, HD, U1, HCP, EU = range(8)
N_HALO = 8
R_FINE1, R_COARSE, R_FINE2, R_CHAIN = range(4)


def kernel(
    sizes,
    state,
    labels,
    rigidity,
    mismatch,
    heat,
    coefs,
    times,
    out,
    lab_x,
    fields,
    kel_b,
    thermal_b,
    sdiag_b,
    inv_fine,
    inv_loose,
    image_b,
    basis,
    part,
    red,
    p_in,
    p_out,
    eu_out,
    u2_b,
    corr_b,
    halo_send,
    halo_recv,
    red_send,
    red_recv,
    tm_send,
    tm_recv,
):
    n_tm, n_gx, n_gy = sizes
    _, prony, nx, ny, nz = state.shape
    prony -= 1
    h = SHARP_SOLVER_ITER + 1
    rows = nx + 2 * h
    wide = ny + 2 * PAD
    tm, gx, gy = lax.axis_index("tm"), lax.axis_index("gx"), lax.axis_index("gy")
    me = gx * n_gy + gy
    own_r = pl.ds(h, nx)
    own_c = pl.ds(PAD, ny)

    def ext(which):
        return lab_x if which == LAB else fields.at[which - 1]

    lab_x[...] = jnp.full(lab_x.shape, -1, jnp.int32)
    zero_row = jnp.zeros((wide, nz), F32)

    def clear(i, carry):
        for which in range(1, N_HALO):
            fields[which - 1, i] = zero_row
        return carry

    lax.fori_loop(0, rows, clear, 0)

    barrier = pltpu.get_barrier_semaphore()
    peers = [(a, b) for a in range(n_gx) for b in range(n_gy)]
    for a, b in peers:

        @pl.when(a * n_gy + b != me)
        def _():
            pl.semaphore_signal(barrier, inc=1, device_id=(tm, a, b), device_id_type=MESH)

    for step in (-1, 1):

        @pl.when((tm + step >= 0) & (tm + step < n_tm))
        def _():
            pl.semaphore_signal(
                barrier, inc=1, device_id=(tm + step, gx, gy), device_id_type=MESH
            )

    def splat(value):
        return jnp.full((1, nz), value, F32)

    def decays(dt):
        decay = [jnp.exp(-dt / splat(times[p])) for p in range(prony)]
        factor = [splat(coefs[p]) * decay[p] for p in range(prony)]
        return decay, factor

    fine_dt, loose_dt = 1.0, 1.0 * PARTITION_PACES
    d_fine, f_fine = decays(fine_dt)
    d_loose, f_loose = decays(loose_dt)
    s_fine = sum(f_fine, splat(1.0 / fine_dt))
    s_loose = sum(f_loose, splat(1.0 / loose_dt))

    def fill(i, carry):
        lab_x[h + i, own_c] = labels[i]
        hist = [state[0, 1 + p, i] for p in range(prony)]
        fields[U0 - 1, h + i, own_c] = state[0, 0, i]
        fields[H1 - 1, h + i, own_c] = sum(f_fine[p] * hist[p] for p in range(prony))
        fields[HC - 1, h + i, own_c] = sum(f_loose[p] * hist[p] for p in range(prony))
        fields[HD - 1, h + i, own_c] = sum(
            f_fine[p] * d_fine[p] * hist[p] for p in range(prony)
        )
        return carry

    lax.fori_loop(0, nx, fill, 0)
    waits = (
        len(peers)
        - 1
        + jnp.where(tm > 0, 1, 0).astype(jnp.int32)
        + jnp.where(tm < n_tm - 1, 1, 0).astype(jnp.int32)
    )
    pl.semaphore_wait(barrier, waits)

    directions = [(a, b) for a in (-1, 0, 1) for b in (-1, 0, 1) if (a, b) != (0, 0)]
    src_r = {-1: pl.ds(h, h), 0: own_r, 1: pl.ds(nx, h)}
    dst_r = {-1: pl.ds(h + nx, h), 0: own_r, 1: pl.ds(0, h)}
    src_c = {-1: pl.ds(PAD, PAD), 0: own_c, 1: pl.ds(ny, PAD)}
    dst_c = {-1: pl.ds(PAD + ny, PAD), 0: own_c, 1: pl.ds(0, PAD)}

    def exists(a, b):
        return (gx + a >= 0) & (gx + a < n_gx) & (gy + b >= 0) & (gy + b < n_gy)

    def halo_copy(which, index):
        a, b = directions[index]
        ref = ext(which)
        return pltpu.make_async_remote_copy(
            src_ref=ref.at[src_r[a], src_c[b]],
            dst_ref=ref.at[dst_r[a], dst_c[b]],
            send_sem=halo_send.at[which, index],
            recv_sem=halo_recv.at[which, index],
            device_id=(tm, gx + a, gy + b),
            device_id_type=MESH,
        )

    def halo_start(*which_all):
        for index, (a, b) in enumerate(directions):

            @pl.when(exists(a, b))
            def _():
                for which in which_all:
                    halo_copy(which, index).start()

    def halo_wait(*which_all):
        for index, (a, b) in enumerate(directions):

            @pl.when(exists(-a, -b))
            def _():
                for which in which_all:
                    halo_copy(which, index).wait_recv()

    def halo_drain(*which_all):
        for index, (a, b) in enumerate(directions):

            @pl.when(exists(a, b))
            def _():
                for which in which_all:
                    halo_copy(which, index).wait_send()

    halo_start(LAB, U0, H1)
    halo_start(HC, HD)

    def red_copy(which, target):
        a, b = peers[target]
        return pltpu.make_async_remote_copy(
            src_ref=part.at[which],
            dst_ref=red.at[which, me],
            send_sem=red_send.at[which, target],
            recv_sem=red_recv.at[which, me],
            device_id=(tm, a, b),
            device_id_type=MESH,
        )

    def red_start(which, sums):
        for j, value in enumerate(sums):
            part[which, j : j + 1] = jnp.sum(value, axis=0, keepdims=True)
        for target in range(len(peers)):

            @pl.when(target != me)
            def _():
                red_copy(which, target).start()

    def red_finish(which, count):
        for source in range(len(peers)):

            @pl.when(source != me)
            def _():
                pltpu.make_async_remote_copy(
                    src_ref=part.at[which],
                    dst_ref=red.at[which, source],
                    send_sem=red_send.at[which, source],
                    recv_sem=red_recv.at[which, source],
                    device_id=(tm, gx, gy),
                    device_id_type=MESH,
                ).wait_recv()

        mine = part[which]
        total = None
        for source in range(len(peers)):
            value = jnp.where(source == me, mine, red[which, source])
            total = value if total is None else total + value
        total = jnp.broadcast_to(jnp.sum(total, axis=1, keepdims=True), total.shape)
        return [total[j : j + 1] for j in range(count)]

    def red_drain(which):
        for target in range(len(peers)):

            @pl.when(target != me)
            def _():
                red_copy(which, target).wait_send()

    lane = lax.broadcasted_iota(jnp.int32, (wide, nz), 1)
    first_lane, last_lane = lane == 0, lane == nz - 1

    def next_z(v):
        return jnp.where(last_lane, 0.0, pltpu.roll(v, nz - 1, 1))

    def prior_z(v):
        return jnp.where(first_lane, 0.0, pltpu.roll(v, 1, 1))

    def next_y(v):
        return pltpu.roll(v, wide - 1, 0)

    def prior_y(v):
        return pltpu.roll(v, 1, 0)

    def forward(v):
        up = next_z(v)
        total, diff = v + up, up - v
        total_up, diff_up = next_y(total), next_y(diff)
        return (total + total_up, diff + diff_up, total_up - total, diff_up - diff)

    def element_row(low, high, k):
        k2 = k + k
        k3 = k2 + k
        g1 = k3 * (high[0] - low[0])
        to_low, to_high = [-g1], [g1]
        for f, weights in ((1, (k3, k2)), (2, (k3, k2)), (3, (k2, k))):
            g0 = weights[0] * (high[f] + low[f])
            g1 = weights[1] * (high[f] - low[f])
            to_low.append(g0 - g1)
            to_high.append(g0 + g1)
        return to_low, to_high

    def backward(g):
        zs = (g[0] - g[2]) + prior_y(g[0] + g[2])
        zd = (g[1] - g[3]) + prior_y(g[1] + g[3])
        return (zs - zd) + prior_z(zs + zd)

    def apply(load, emit, margin, extra):
        low_row, high_row = h - margin, h + nx + margin
        before = forward(load(low_row - 1))
        here = forward(load(low_row))
        _, pending = element_row(before, here, kel_b[low_row - 1])

        def body(e, carry):
            here, pending, extra = carry
            after = forward(load(e + 1))
            to_low, to_high = element_row(here, after, kel_b[e])
            image = backward([x + y for x, y in zip(pending, to_low)])
            extra = emit(e, image, extra)
            return after, tuple(to_high), extra

        _, _, extra = lax.fori_loop(
            low_row, high_row, body, (here, tuple(pending), extra), unroll=UNROLL
        )
        return extra

    zero_sum = jnp.zeros((ny, nz), F32)

    def own(v):
        return v[PAD : PAD + ny]

    def own_weight(e):
        return jnp.where((e >= h) & (e < h + nx), 1.0, 0.0).astype(F32)

    def krylov(iterations, inv_b, level0):
        sums = [level0]
        for k in range(iterations):
            final = k + 1 == iterations

            def emit(e, image, carry):
                v = basis[k, e]
                t = image - sdiag_b[e] * v
                if final:
                    return (carry[0] + own(v * t),)
                v_new = inv_b[e] * t
                basis[k + 1, e] = v_new
                w = own_weight(e)
                t = own(t) * w
                return carry[0] + own(v) * t, carry[1] + own(v_new) * t

            count = 1 if final else 2
            got = apply(
                lambda e: basis[k, e], emit, iterations - 1 - k, (zero_sum,) * count
            )
            sums.extend(got)
        return sums

    def first_level(u_ref, h_ref, u_weight, level, inv_b, margin, keep_image):
        def emit(e, image, carry):
            if keep_image:
                image_b[e] = image
            r = u_weight * u_ref[e] + level * thermal_b[e] + h_ref[e] - image
            v = inv_b[e] * r
            basis[0, e] = v
            return (carry[0] + own(v * r) * own_weight(e),)

        return apply(lambda e: u_ref[e], emit, margin, (zero_sum,))[0]

    def guarded(numerator, denominator):
        good = denominator > 0.0
        return jnp.where(good, numerator / jnp.where(good, denominator, 1.0), 0.0)

    def galerkin(nu, m):
        a = [nu[j] + nu[j + 1] for j in range(2 * m - 1)]
        lower = [[None] * m for _ in range(m)]
        pivots, y = [], []
        for i in range(m):
            row = []
            for j in range(i):
                value = a[i + j]
                for q in range(j):
                    value = value - row[q] * lower[j][q]
                row.append(value)
                lower[i][j] = guarded(value, pivots[j])
            pivot, rhs = a[2 * i], nu[i]
            for q in range(i):
                pivot = pivot - row[q] * lower[i][q]
                rhs = rhs - lower[i][q] * y[q]
            pivots.append(pivot)
            y.append(rhs)
        c = [None] * m
        for i in reversed(range(m)):
            value = guarded(y[i], pivots[i])
            for q in range(i + 1, m):
                value = value - lower[q][i] * c[q]
            c[i] = value
        return c

    def solved(u, c, i):
        for k, weight in enumerate(c):
            u = u + weight * basis[k, h + i, own_c]
        return u

    halo_wait(LAB, U0, H1)
    node_y = gy * ny - PAD + lax.broadcasted_iota(jnp.int32, (wide, nz), 0)
    inside_y = (node_y >= 0) & (node_y < n_gy * ny)

    def coefficients(e):
        ids = lab_x[e]
        kel = jnp.zeros((wide, nz), F32)
        gap = jnp.zeros((wide, nz), F32)
        for region in range(rigidity.shape[0]):
            here = ids == region
            kel = jnp.where(here, rigidity[region], kel)
            gap = jnp.where(here, mismatch[region], gap)
        kal = kel * gap
        return kel, kal

    def nodal(kel, kal):
        kel_y = kel + prior_y(kel)
        kal_y = kal + prior_y(kal)
        return kel_y + prior_z(kel_y), prior_z(kal_y) - kal_y

    kel, kal = coefficients(0)
    kel_b[0] = kel * (1.0 / 48.0)

    def setup(e, carry):
        kel, kal = coefficients(e)
        kel_b[e] = kel * (1.0 / 48.0)
        new = nodal(kel, kal)
        diag = (carry[0] + new[0]) * (1.0 / 3.0)
        sdiag_b[e] = diag
        thermal_b[e] = (carry[1] + new[1]) * 0.25
        node_x = gx * nx - h + e
        inside = jnp.where((node_x >= 0) & (node_x < n_gx * nx), 1.0, 0.0).astype(F32)
        inv_fine[e] = jnp.where(inside_y, inside / (s_fine + diag), 0.0)
        inv_loose[e] = jnp.where(inside_y, inside / (s_loose + diag), 0.0)
        return new

    lax.fori_loop(1, rows, setup, nodal(kel, kal))

    heat_fine = [splat(heat[0, s]) for s in range(PARTITION_PACES)]
    heat_loose = heat_fine[PARTITION_PACES - 1]
    u0_x, u1_x, eu_x = ext(U0), ext(U1), ext(EU)

    level0 = first_level(
        u0_x,
        ext(H1),
        splat(1.0 / fine_dt) - s_fine,
        heat_fine[0],
        inv_fine,
        SHARP_SOLVER_ITER,
        True,
    )
    red_start(R_FINE1, krylov(SHARP_SOLVER_ITER, inv_fine, level0))
    c = galerkin(red_finish(R_FINE1, 2 * SHARP_SOLVER_ITER), SHARP_SOLVER_ITER)

    def end_fine1(i, carry):
        fields[U1 - 1, h + i, own_c] = solved(u0_x[h + i, own_c], c, i)
        return carry

    lax.fori_loop(0, nx, end_fine1, 0)
    halo_start(U1)

    halo_wait(HC, HD)
    h_coarse = ext(HC)

    def coarse_first(e, carry):
        r = (
            (splat(1.0 / loose_dt) - s_loose) * u0_x[e]
            + heat_loose * thermal_b[e]
            + h_coarse[e]
            - image_b[e]
        )
        v = inv_loose[e] * r
        basis[0, e] = v
        return carry + own(v * r) * own_weight(e)

    level0 = lax.fori_loop(
        h - LOOSE_SOLVER_ITER, h + nx + LOOSE_SOLVER_ITER, coarse_first, zero_sum
    )
    red_start(R_COARSE, krylov(LOOSE_SOLVER_ITER, inv_loose, level0))
    c = galerkin(red_finish(R_COARSE, 2 * LOOSE_SOLVER_ITER), LOOSE_SOLVER_ITER)

    keep_fine = [1.0 - d for d in d_fine]
    keep_loose = [1.0 - d for d in d_loose]

    def end_coarse(i, carry):
        u = solved(u0_x[h + i, own_c], c, i)
        corr_b[0, i] = -u
        u1 = u1_x[h + i, own_c]
        for p in range(prony):
            old = state[0, 1 + p, i]
            corr_b[1 + p, i] = -(d_loose[p] * old + keep_loose[p] * u)
            p_out[p, i] = d_fine[p] * (d_fine[p] * old + keep_fine[p] * u1)
        return carry

    lax.fori_loop(0, nx, end_coarse, 0)

    def tm_copy(index, up):
        src = eu_out if index == prony else p_out.at[index]
        dst = eu_x.at[own_r, own_c] if index == prony else p_in.at[index]
        return pltpu.make_async_remote_copy(
            src_ref=src,
            dst_ref=dst,
            send_sem=tm_send.at[index],
            recv_sem=tm_recv.at[index],
            device_id=(tm + up, gx, gy),
            device_id_type=MESH,
        )

    has_next = tm < n_tm - 1

    @pl.when((tm == 0) & has_next)
    def _():
        for p in range(prony):
            tm_copy(p, 1).start()

    halo_wait(U1)
    held = sum((f_fine[p] * d_fine[p] for p in range(prony)), splat(0.0))
    level0 = first_level(
        u1_x, ext(HD), -held, heat_fine[1], inv_fine, SHARP_SOLVER_ITER, False
    )
    red_start(R_FINE2, krylov(SHARP_SOLVER_ITER, inv_fine, level0))
    c_fine = galerkin(red_finish(R_FINE2, 2 * SHARP_SOLVER_ITER), SHARP_SOLVER_ITER)

    @pl.when(tm == 0)
    def _():
        def first_u(i, carry):
            eu_out[i] = solved(u1_x[h + i, own_c], c_fine, i)
            return carry

        lax.fori_loop(0, nx, first_u, 0)

        @pl.when(has_next)
        def _():
            tm_copy(prony, 1).start()

        def first_out(i, carry):
            u2 = eu_out[i]
            out[0, 0, i] = u2
            for p in range(prony):
                out[0, 1 + p, i] = p_out[p, i] + keep_fine[p] * u2
            return carry

        lax.fori_loop(0, nx, first_out, 0)

    @pl.when(tm > 0)
    def _():
        def correct(i, carry):
            u2 = solved(u1_x[h + i, own_c], c_fine, i)
            corr_b[0, i] = corr_b[0, i] + u2
            for p in range(prony):
                corr_b[1 + p, i] = corr_b[1 + p, i] + (p_out[p, i] + keep_fine[p] * u2)
            return carry

        lax.fori_loop(0, nx, correct, 0)

        from_first = tm == 1
        given = [jnp.where(from_first, keep_fine[p], keep_loose[p]) for p in range(prony)]
        for p in range(prony):
            tm_copy(p, -1).wait_recv()

        def combine(i, carry):
            fields[HCP - 1, h + i, own_c] = sum(f_loose[p] * p_in[p, i] for p in range(prony))
            return carry

        lax.fori_loop(0, nx, combine, 0)
        halo_start(HCP)
        tm_copy(prony, -1).wait_recv()
        halo_start(EU)

        def ahead(i, carry):
            u = eu_x[h + i, own_c]
            for p in range(prony):
                old = p_in[p, i] + given[p] * u
                p_out[p, i] = (
                    d_loose[p] * old + corr_b[1 + p, i] - keep_loose[p] * corr_b[0, i]
                )
            return carry

        lax.fori_loop(0, nx, ahead, 0)

        @pl.when(has_next)
        def _():
            for p in range(prony):
                tm_copy(p, 1).start()

        halo_wait(HCP, EU)
        gain = splat(1.0 / loose_dt) - s_loose
        for p in range(prony):
            gain = gain + f_loose[p] * given[p]
        level0 = first_level(
            eu_x, ext(HCP), gain, heat_loose, inv_loose, LOOSE_SOLVER_ITER, False
        )
        red_start(R_CHAIN, krylov(LOOSE_SOLVER_ITER, inv_loose, level0))
        c = galerkin(red_finish(R_CHAIN, 2 * LOOSE_SOLVER_ITER), LOOSE_SOLVER_ITER)

        def last_u(i, carry):
            eu_out[i] = solved(eu_x[h + i, own_c], c, i) + corr_b[0, i]
            return carry

        lax.fori_loop(0, nx, last_u, 0)

        @pl.when(has_next)
        def _():
            tm_copy(prony, 1).start()

        def last_out(i, carry):
            u = eu_out[i]
            out[0, 0, i] = u
            for p in range(prony):
                out[0, 1 + p, i] = p_out[p, i] + keep_loose[p] * u
            return carry

        lax.fori_loop(0, nx, last_out, 0)
        halo_drain(HCP, EU)
        red_drain(R_CHAIN)

    @pl.when(has_next)
    def _():
        for index in range(prony + 1):
            tm_copy(index, 1).wait_send()

    halo_drain(LAB, U0, H1, HC, HD, U1)
    for which in (R_FINE1, R_COARSE, R_FINE2):
        red_drain(which)


def on_device(sizes, state, labels, rigidity, mismatch, heat, coefs, times):
    _, fields, nx, ny, nz = state.shape
    h = SHARP_SOLVER_ITER + 1
    rows, wide = nx + 2 * h, ny + 2 * PAD
    peers = sizes[1] * sizes[2]
    field = (rows, wide, nz)
    own = (nx, ny, nz)
    vmem = pl.BlockSpec(memory_space=pltpu.VMEM)
    smem = pl.BlockSpec(memory_space=pltpu.SMEM)
    dma = pltpu.SemaphoreType.DMA
    return pl.pallas_call(
        functools.partial(kernel, sizes),
        out_shape=jax.ShapeDtypeStruct(state.shape, state.dtype),
        in_specs=[vmem, vmem, smem, smem, smem, smem, smem],
        out_specs=vmem,
        scratch_shapes=[
            pltpu.VMEM(field, jnp.int32),
            pltpu.VMEM((N_HALO - 1,) + field, F32),
            pltpu.VMEM(field, F32),
            pltpu.VMEM(field, F32),
            pltpu.VMEM(field, F32),
            pltpu.VMEM(field, F32),
            pltpu.VMEM(field, F32),
            pltpu.VMEM(field, F32),
            pltpu.VMEM((SHARP_SOLVER_ITER,) + field, F32),
            pltpu.VMEM((4, 8, nz), F32),
            pltpu.VMEM((4, peers, 8, nz), F32),
            pltpu.VMEM((fields - 1,) + own, F32),
            pltpu.VMEM((fields - 1,) + own, F32),
            pltpu.VMEM(own, F32),
            pltpu.VMEM(own, F32),
            pltpu.VMEM((fields,) + own, F32),
            dma((N_HALO, 8)),
            dma((N_HALO, 8)),
            dma((4, peers)),
            dma((4, peers)),
            dma((fields,)),
            dma((fields,)),
        ],
        compiler_params=pltpu.CompilerParams(
            collective_id=0, has_side_effects=True, vmem_limit_bytes=56 * 1024 * 1024
        ),
    )(state, labels, rigidity, mismatch, heat, coefs, times)


def solution(mesh):
    sizes = tuple(mesh.shape[name] for name in ("tm", "gx", "gy"))
    placed = (
        P("tm", None, "gx", "gy", None),
        P("gx", "gy", None),
        P(),
        P(),
        P("tm", None),
        P(),
        P(),
    )
    return jax.shard_map(
        functools.partial(on_device, sizes),
        mesh=mesh,
        in_specs=placed,
        out_specs=P("tm", None, "gx", "gy", None),
        check_vma=False,
    )
```

time: 557 us -> 84.1 us (0.15)
  starting transfers between devices: 217 us -> 0 us
  blocking collectives: 141 us -> 0 us
  Pallas kernels: 0 us -> 82.2 us
  waiting for transfers between devices: 79.3 us -> 0 us
  other arithmetic: 54.4 us -> 0 us
  between operations: 26.8 us -> 0.01 us
  loops' own time: 19.1 us -> 0 us
  local copies, waits for them, and re-layouts: 14.9 us -> 1.77 us
    ppermute x81 -> x0, starting transfers between devices: 217 us -> none  [the longest x38 123 us: padded_2(): lax.ppermute(lax.slice_in_dim(block, block.shape[dim] - width, None, axis...]
    psum x12 -> x0, blocking collectives: 141 us -> none  [pair_sum(): lax.psum((inner_sum(remainder, scaled), inner_sum(image, scaled)), ('gx',...]
    pallas_call x0 -> x1, Pallas kernels: none -> 82.2 us  [on_device(): pl.pallas_call(functools.partial(kernel, sizes), out_shape=jax.ShapeDtype...]
    ppermute x81 -> x0, waiting for transfers between devices: 79.3 us -> none  [the longest x38 43.1 us: padded_2(): lax.ppermute(lax.slice_in_dim(block, 0, width, axis=dim), axis, backward)]
    reduce_sum x28 -> x0, other arithmetic: 25.5 us -> none  [the longest x19 21.7 us: inner_sum(): return jnp.sum(left * right)]
    another operation x1 -> x0, loops' own time: 19.1 us -> none  [on_device(): finished = lax.fori_loop(0, lax.axis_size('tm') - 1, next_turn, finished)]
    select_n x11 -> x0, other arithmetic: 15.4 us -> none  [the longest x7 7.76 us: conjugate_solve(): scaled = jnp.where(node_inside, remainder / diagonal, 0.0)]
    slice x46 -> x0, local copies, waits for them, and re-layouts: 10.5 us -> none  [the longest x19 5.1 us: stencil_apply(): padded[near_one:near_one + extent_one, near_two:near_two + extent_two, ne...]
  transfers between devices with their start and end apart: 81 -> 0, of which waited for: 33 -> 0; matrix products, arithmetic and copies ran while one was open for 4% -> 0% of each run, Pallas kernels for 0% -> 0%
where the time goes in v1:
time: 84.1 us; the launch traced here: 83.9 us
  Pallas kernels  82.2 us (98%)
  local copies, waits for them, and re-layouts  1.77 us (2%)
    pallas_call x1, Pallas kernels, on_device(): pl.pallas_call(functools.partial(kernel, sizes), out_shape=jax.ShapeDtype...  82.2 us
    unnamed x1, local copies, waits for them, and re-layouts  1.77 us

profile of v1, /device:TPU:25, one launch (start us, length us, event | category | flops | bytes accessed | tf_op | source)
XLA Modules:
  0.0 83.9 jit_solution(9481595817246656272)
XLA Ops:
  0.0 82.2 %shard_map.73 = f32[1,4,12,16,128]{4,3,2,1,0:T(8,128)} custom-call(f32[1,4,12,16,128]{4,3,2,1,0:T(8,128)} %state.1, s32[12,16,128]{2,1,0:T(8,128)} %labels.1, f32[6]{0:T(128)} %rigidity.1, f32[6]{0:T(128)} %mismatch.1, f32[1,2]{1,0:T(1,128)} %heat.1, f32[3]{0:T(128)} %coefs.1, f32[3]{0:T(128)} %times.1), custom_call_target="tpu_custom_call" | custom-call | tf_op jit(solution)/shard_map/pallas_call | solution.py:597
  82.2 1.8 %copy.9 = f32[1,4,12,16,128]{4,3,2,1,0:T(8,128)} copy(f32[1,4,12,16,128]{4,3,2,1,0:T(8,128)} %shard_map.73) | data formatting | bytes 786432

commit v2 on v1

--- a/solution.py
+++ b/solution.py
@@ -13,11 +13,34 @@
 MESH = pl.DeviceIdType.MESH
 F32 = jnp.float32
 PAD = 8
-UNROLL = 2
+UNROLL = 4
 
 LAB, U0, H1, HC, HD, U1, HCP, EU = range(8)
 N_HALO = 8
+FINE_RIM, LOOSE_RIM = SHARP_SOLVER_ITER + 1, LOOSE_SOLVER_ITER + 1
+RIM = {
+    LAB: FINE_RIM,
+    U0: FINE_RIM,
+    H1: FINE_RIM - 1,
+    HC: LOOSE_RIM - 1,
+    HD: FINE_RIM - 1,
+    U1: FINE_RIM,
+    HCP: LOOSE_RIM - 1,
+    EU: LOOSE_RIM,
+}
 R_FINE1, R_COARSE, R_FINE2, R_CHAIN = range(4)
+
+
+def chunks_of(nx):
+    middle = nx - 2 * LOOSE_RIM
+    cut = [(0, LOOSE_RIM), (nx - LOOSE_RIM, LOOSE_RIM)]
+    half = middle // 2
+    cut += [(LOOSE_RIM, half), (LOOSE_RIM + half, middle - half)]
+    return [(start, count) for start, count in cut if count > 0]
+
+
+def loop(low, high, body, carry):
+    return lax.fori_loop(low, high, body, carry, unroll=UNROLL)
 
 
 def kernel(
@@ -39,6 +62,7 @@
     inv_loose,
     image_b,
     basis,
+    basis_loose,
     part,
     red,
     p_in,
@@ -52,6 +76,8 @@
     red_recv,
     tm_send,
     tm_recv,
+    side_send,
+    side_recv,
 ):
     n_tm, n_gx, n_gy = sizes
     _, prony, nx, ny, nz = state.shape
@@ -75,7 +101,12 @@
             fields[which - 1, i] = zero_row
         return carry
 
-    lax.fori_loop(0, rows, clear, 0)
+    loop(0, rows, clear, 0)
+    for row in (h - 1, h + nx):
+        for k in range(SHARP_SOLVER_ITER):
+            basis[k, row] = zero_row
+        for k in range(LOOSE_SOLVER_ITER):
+            basis_loose[k, row] = zero_row
 
     barrier = pltpu.get_barrier_semaphore()
     peers = [(a, b) for a in range(n_gx) for b in range(n_gy)]
@@ -118,7 +149,7 @@
         )
         return carry
 
-    lax.fori_loop(0, nx, fill, 0)
+    loop(0, nx, fill, 0)
     waits = (
         len(peers)
         - 1
@@ -128,8 +159,13 @@
     pl.semaphore_wait(barrier, waits)
 
     directions = [(a, b) for a in (-1, 0, 1) for b in (-1, 0, 1) if (a, b) != (0, 0)]
-    src_r = {-1: pl.ds(h, h), 0: own_r, 1: pl.ds(nx, h)}
-    dst_r = {-1: pl.ds(h + nx, h), 0: own_r, 1: pl.ds(0, h)}
+
+    def src_r(a, w):
+        return {-1: pl.ds(h, w), 0: own_r, 1: pl.ds(h + nx - w, w)}[a]
+
+    def dst_r(a, w):
+        return {-1: pl.ds(h + nx, w), 0: own_r, 1: pl.ds(h - w, w)}[a]
+
     src_c = {-1: pl.ds(PAD, PAD), 0: own_c, 1: pl.ds(ny, PAD)}
     dst_c = {-1: pl.ds(PAD + ny, PAD), 0: own_c, 1: pl.ds(0, PAD)}
 
@@ -140,8 +176,8 @@
         a, b = directions[index]
         ref = ext(which)
         return pltpu.make_async_remote_copy(
-            src_ref=ref.at[src_r[a], src_c[b]],
-            dst_ref=ref.at[dst_r[a], dst_c[b]],
+            src_ref=ref.at[src_r(a, RIM[which]), src_c[b]],
+            dst_ref=ref.at[dst_r(a, RIM[which]), dst_c[b]],
             send_sem=halo_send.at[which, index],
             recv_sem=halo_recv.at[which, index],
             device_id=(tm, gx + a, gy + b),
@@ -262,14 +298,22 @@
         zd = (g[1] - g[3]) + prior_y(g[1] + g[3])
         return (zs - zd) + prior_z(zs + zd)
 
+    def span(margin):
+        if n_gx == 1:
+            return h, nx
+        if n_gx == 2:
+            return h - margin * gx, nx + margin
+        return h - margin, nx + 2 * margin
+
     def apply(load, emit, margin, extra):
-        low_row, high_row = h - margin, h + nx + margin
+        low_row, count = span(margin)
         before = forward(load(low_row - 1))
         here = forward(load(low_row))
         _, pending = element_row(before, here, kel_b[low_row - 1])
 
-        def body(e, carry):
+        def body(t, carry):
             here, pending, extra = carry
+            e = low_row + t
             after = forward(load(e + 1))
             to_low, to_high = element_row(here, after, kel_b[e])
             image = backward([x + y for x, y in zip(pending, to_low)])
@@ -277,7 +321,7 @@
             return after, tuple(to_high), extra
 
         _, _, extra = lax.fori_loop(
-            low_row, high_row, body, (here, tuple(pending), extra), unroll=UNROLL
+            0, count, body, (here, tuple(pending), extra), unroll=True
         )
         return extra
 
@@ -289,7 +333,7 @@
     def own_weight(e):
         return jnp.where((e >= h) & (e < h + nx), 1.0, 0.0).astype(F32)
 
-    def krylov(iterations, inv_b, level0):
+    def krylov(iterations, basis, inv_b, level0):
         sums = [level0]
         for k in range(iterations):
             final = k + 1 == iterations
@@ -353,7 +397,7 @@
             c[i] = value
         return c
 
-    def solved(u, c, i):
+    def solved(u, c, i, basis=basis):
         for k, weight in enumerate(c):
             u = u + weight * basis[k, h + i, own_c]
         return u
@@ -394,7 +438,7 @@
         inv_loose[e] = jnp.where(inside_y, inside / (s_loose + diag), 0.0)
         return new
 
-    lax.fori_loop(1, rows, setup, nodal(kel, kal))
+    loop(1, rows, setup, nodal(kel, kal))
 
     heat_fine = [splat(heat[0, s]) for s in range(PARTITION_PACES)]
     heat_loose = heat_fine[PARTITION_PACES - 1]
@@ -409,20 +453,14 @@
         SHARP_SOLVER_ITER,
         True,
     )
-    red_start(R_FINE1, krylov(SHARP_SOLVER_ITER, inv_fine, level0))
-    c = galerkin(red_finish(R_FINE1, 2 * SHARP_SOLVER_ITER), SHARP_SOLVER_ITER)
-
-    def end_fine1(i, carry):
-        fields[U1 - 1, h + i, own_c] = solved(u0_x[h + i, own_c], c, i)
-        return carry
-
-    lax.fori_loop(0, nx, end_fine1, 0)
-    halo_start(U1)
-
-    halo_wait(HC, HD)
+    red_start(R_FINE1, krylov(SHARP_SOLVER_ITER, basis, inv_fine, level0))
+
+    halo_wait(HC)
     h_coarse = ext(HC)
-
-    def coarse_first(e, carry):
+    coarse_low, coarse_count = span(LOOSE_SOLVER_ITER)
+
+    def coarse_first(t, carry):
+        e = coarse_low + t
         r = (
             (splat(1.0 / loose_dt) - s_loose) * u0_x[e]
             + heat_loose * thermal_b[e]
@@ -430,33 +468,43 @@
             - image_b[e]
         )
         v = inv_loose[e] * r
-        basis[0, e] = v
+        basis_loose[0, e] = v
         return carry + own(v * r) * own_weight(e)
 
-    level0 = lax.fori_loop(
-        h - LOOSE_SOLVER_ITER, h + nx + LOOSE_SOLVER_ITER, coarse_first, zero_sum
-    )
-    red_start(R_COARSE, krylov(LOOSE_SOLVER_ITER, inv_loose, level0))
-    c = galerkin(red_finish(R_COARSE, 2 * LOOSE_SOLVER_ITER), LOOSE_SOLVER_ITER)
+    level0 = loop(0, coarse_count, coarse_first, zero_sum)
+    red_start(R_COARSE, krylov(LOOSE_SOLVER_ITER, basis_loose, inv_loose, level0))
+
+    c = galerkin(red_finish(R_FINE1, 2 * SHARP_SOLVER_ITER), SHARP_SOLVER_ITER)
+
+    def end_fine1(i, carry):
+        fields[U1 - 1, h + i, own_c] = solved(u0_x[h + i, own_c], c, i)
+        return carry
+
+    loop(0, nx, end_fine1, 0)
+    halo_start(U1)
 
     keep_fine = [1.0 - d for d in d_fine]
     keep_loose = [1.0 - d for d in d_loose]
 
-    def end_coarse(i, carry):
-        u = solved(u0_x[h + i, own_c], c, i)
-        corr_b[0, i] = -u
+    def give_fine(i, carry):
         u1 = u1_x[h + i, own_c]
         for p in range(prony):
-            old = state[0, 1 + p, i]
-            corr_b[1 + p, i] = -(d_loose[p] * old + keep_loose[p] * u)
-            p_out[p, i] = d_fine[p] * (d_fine[p] * old + keep_fine[p] * u1)
+            p_out[p, i] = d_fine[p] * (
+                d_fine[p] * state[0, 1 + p, i] + keep_fine[p] * u1
+            )
         return carry
 
-    lax.fori_loop(0, nx, end_coarse, 0)
+    loop(0, nx, give_fine, 0)
+
+    chunks = chunks_of(nx)
 
     def tm_copy(index, up):
-        src = eu_out if index == prony else p_out.at[index]
-        dst = eu_x.at[own_r, own_c] if index == prony else p_in.at[index]
+        if index < prony:
+            src, dst = p_out.at[index], p_in.at[index]
+        else:
+            start, count = chunks[index - prony]
+            src = eu_out.at[pl.ds(start, count)]
+            dst = eu_x.at[pl.ds(h + start, count), own_c]
         return pltpu.make_async_remote_copy(
             src_ref=src,
             dst_ref=dst,
@@ -466,6 +514,49 @@
             device_id_type=MESH,
         )
 
+    def side_copy(index, side):
+        start, count = chunks[index]
+        b = (-1, 1)[side]
+        at = pl.ds(h + start, count)
+        return pltpu.make_async_remote_copy(
+            src_ref=eu_x.at[at, src_c[b]],
+            dst_ref=eu_x.at[at, dst_c[b]],
+            send_sem=side_send.at[index, side],
+            recv_sem=side_recv.at[index, side],
+            device_id=(tm, gx, gy + b),
+            device_id_type=MESH,
+        )
+
+    def end_wait():
+        for side, b in enumerate((-1, 1)):
+
+            @pl.when(exists(0, -b))
+            def _():
+                for index in range(len(chunks)):
+                    side_copy(index, side).wait_recv()
+
+        for corner, (a, b) in enumerate(directions):
+            if a != 0:
+
+                @pl.when(exists(-a, -b))
+                def _():
+                    halo_copy(EU, corner).wait_recv()
+
+    def end_drain():
+        for side, b in enumerate((-1, 1)):
+
+            @pl.when(exists(0, b))
+            def _():
+                for index in range(len(chunks)):
+                    side_copy(index, side).wait_send()
+
+        for corner, (a, b) in enumerate(directions):
+            if a != 0:
+
+                @pl.when(exists(a, b))
+                def _():
+                    halo_copy(EU, corner).wait_send()
+
     has_next = tm < n_tm - 1
 
     @pl.when((tm == 0) & has_next)
@@ -473,12 +564,23 @@
         for p in range(prony):
             tm_copy(p, 1).start()
 
-    halo_wait(U1)
+    c = galerkin(red_finish(R_COARSE, 2 * LOOSE_SOLVER_ITER), LOOSE_SOLVER_ITER)
+
+    def end_coarse(i, carry):
+        u = solved(u0_x[h + i, own_c], c, i, basis_loose)
+        corr_b[0, i] = -u
+        for p in range(prony):
+            corr_b[1 + p, i] = -(d_loose[p] * state[0, 1 + p, i] + keep_loose[p] * u)
+        return carry
+
+    loop(0, nx, end_coarse, 0)
+
+    halo_wait(HD, U1)
     held = sum((f_fine[p] * d_fine[p] for p in range(prony)), splat(0.0))
     level0 = first_level(
         u1_x, ext(HD), -held, heat_fine[1], inv_fine, SHARP_SOLVER_ITER, False
     )
-    red_start(R_FINE2, krylov(SHARP_SOLVER_ITER, inv_fine, level0))
+    red_start(R_FINE2, krylov(SHARP_SOLVER_ITER, basis, inv_fine, level0))
     c_fine = galerkin(red_finish(R_FINE2, 2 * SHARP_SOLVER_ITER), SHARP_SOLVER_ITER)
 
     @pl.when(tm == 0)
@@ -487,11 +589,12 @@
             eu_out[i] = solved(u1_x[h + i, own_c], c_fine, i)
             return carry
 
-        lax.fori_loop(0, nx, first_u, 0)
-
-        @pl.when(has_next)
-        def _():
-            tm_copy(prony, 1).start()
+        for index, (start, count) in enumerate(chunks):
+            loop(start, start + count, first_u, 0)
+
+            @pl.when(has_next)
+            def _():
+                tm_copy(prony + index, 1).start()
 
         def first_out(i, carry):
             u2 = eu_out[i]
@@ -500,7 +603,7 @@
                 out[0, 1 + p, i] = p_out[p, i] + keep_fine[p] * u2
             return carry
 
-        lax.fori_loop(0, nx, first_out, 0)
+        loop(0, nx, first_out, 0)
 
     @pl.when(tm > 0)
     def _():
@@ -511,7 +614,7 @@
                 corr_b[1 + p, i] = corr_b[1 + p, i] + (p_out[p, i] + keep_fine[p] * u2)
             return carry
 
-        lax.fori_loop(0, nx, correct, 0)
+        loop(0, nx, correct, 0)
 
         from_first = tm == 1
         given = [jnp.where(from_first, keep_fine[p], keep_loose[p]) for p in range(prony)]
@@ -522,10 +625,23 @@
             fields[HCP - 1, h + i, own_c] = sum(f_loose[p] * p_in[p, i] for p in range(prony))
             return carry
 
-        lax.fori_loop(0, nx, combine, 0)
+        loop(0, nx, combine, 0)
         halo_start(HCP)
-        tm_copy(prony, -1).wait_recv()
-        halo_start(EU)
+        for index in range(len(chunks)):
+            tm_copy(prony + index, -1).wait_recv()
+            for side, b in enumerate((-1, 1)):
+
+                @pl.when(exists(0, b))
+                def _():
+                    side_copy(index, side).start()
+
+            if index < 2:
+                for corner, (a, b) in enumerate(directions):
+                    if a == (-1, 1)[index]:
+
+                        @pl.when(exists(a, b))
+                        def _():
+                            halo_copy(EU, corner).start()
 
         def ahead(i, carry):
             u = eu_x[h + i, own_c]
@@ -536,32 +652,34 @@
                 )
             return carry
 
-        lax.fori_loop(0, nx, ahead, 0)
+        loop(0, nx, ahead, 0)
 
         @pl.when(has_next)
         def _():
             for p in range(prony):
                 tm_copy(p, 1).start()
 
-        halo_wait(HCP, EU)
+        halo_wait(HCP)
+        end_wait()
         gain = splat(1.0 / loose_dt) - s_loose
         for p in range(prony):
             gain = gain + f_loose[p] * given[p]
         level0 = first_level(
             eu_x, ext(HCP), gain, heat_loose, inv_loose, LOOSE_SOLVER_ITER, False
         )
-        red_start(R_CHAIN, krylov(LOOSE_SOLVER_ITER, inv_loose, level0))
+        red_start(R_CHAIN, krylov(LOOSE_SOLVER_ITER, basis, inv_loose, level0))
         c = galerkin(red_finish(R_CHAIN, 2 * LOOSE_SOLVER_ITER), LOOSE_SOLVER_ITER)
 
         def last_u(i, carry):
             eu_out[i] = solved(eu_x[h + i, own_c], c, i) + corr_b[0, i]
             return carry
 
-        lax.fori_loop(0, nx, last_u, 0)
-
-        @pl.when(has_next)
-        def _():
-            tm_copy(prony, 1).start()
+        for index, (start, count) in enumerate(chunks):
+            loop(start, start + count, last_u, 0)
+
+            @pl.when(has_next)
+            def _():
+                tm_copy(prony + index, 1).start()
 
         def last_out(i, carry):
             u = eu_out[i]
@@ -570,13 +688,14 @@
                 out[0, 1 + p, i] = p_out[p, i] + keep_loose[p] * u
             return carry
 
-        lax.fori_loop(0, nx, last_out, 0)
-        halo_drain(HCP, EU)
+        loop(0, nx, last_out, 0)
+        halo_drain(HCP)
+        end_drain()
         red_drain(R_CHAIN)
 
     @pl.when(has_next)
     def _():
-        for index in range(prony + 1):
+        for index in range(prony + len(chunks)):
             tm_copy(index, 1).wait_send()
 
     halo_drain(LAB, U0, H1, HC, HD, U1)
@@ -589,6 +708,7 @@
     h = SHARP_SOLVER_ITER + 1
     rows, wide = nx + 2 * h, ny + 2 * PAD
     peers = sizes[1] * sizes[2]
+    steps = len(chunks_of(nx))
     field = (rows, wide, nz)
     own = (nx, ny, nz)
     vmem = pl.BlockSpec(memory_space=pltpu.VMEM)
@@ -609,6 +729,7 @@
             pltpu.VMEM(field, F32),
             pltpu.VMEM(field, F32),
             pltpu.VMEM((SHARP_SOLVER_ITER,) + field, F32),
+            pltpu.VMEM((LOOSE_SOLVER_ITER,) + field, F32),
             pltpu.VMEM((4, 8, nz), F32),
             pltpu.VMEM((4, peers, 8, nz), F32),
             pltpu.VMEM((fields - 1,) + own, F32),
@@ -620,8 +741,10 @@
             dma((N_HALO, 8)),
             dma((4, peers)),
             dma((4, peers)),
-            dma((fields,)),
-            dma((fields,)),
+            dma((fields - 1 + steps,)),
+            dma((fields - 1 + steps,)),
+            dma((steps, 2)),
+            dma((steps, 2)),
         ],
         compiler_params=pltpu.CompilerParams(
             collective_id=0, has_side_effects=True, vmem_limit_bytes=56 * 1024 * 1024

time: 84.1 us -> 60.4 us (0.72)
  Pallas kernels: 82.2 us -> 58.4 us
    pallas_call x1, Pallas kernels: 82.2 us -> 58.4 us  [on_device(): pl.pallas_call(functools.partial(kernel, sizes), out_shape=jax.ShapeDtype...]
where the time goes in v2:
time: 60.4 us; the launch traced here: 60.2 us
  Pallas kernels  58.4 us (97%)
  local copies, waits for them, and re-layouts  1.77 us (3%)
    pallas_call x1, Pallas kernels, on_device(): pl.pallas_call(functools.partial(kernel, sizes), out_shape=jax.ShapeDtype...  58.4 us
    unnamed x1, local copies, waits for them, and re-layouts  1.77 us

profile of v2, /device:TPU:25, one launch (start us, length us, event | category | flops | bytes accessed | tf_op | source)
XLA Modules:
  0.0 60.2 jit_solution(12418661119588998144)
XLA Ops:
  0.0 58.4 %shard_map.73 = f32[1,4,12,16,128]{4,3,2,1,0:T(8,128)} custom-call(f32[1,4,12,16,128]{4,3,2,1,0:T(8,128)} %state.1, s32[12,16,128]{2,1,0:T(8,128)} %labels.1, f32[6]{0:T(128)} %rigidity.1, f32[6]{0:T(128)} %mismatch.1, f32[1,2]{1,0:T(1,128)} %heat.1, f32[3]{0:T(128)} %coefs.1, f32[3]{0:T(128)} %times.1), custom_call_target="tpu_custom_call" | custom-call | tf_op jit(solution)/shard_map/pallas_call | solution.py:717
  58.4 1.8 %copy.9 = f32[1,4,12,16,128]{4,3,2,1,0:T(8,128)} copy(f32[1,4,12,16,128]{4,3,2,1,0:T(8,128)} %shard_map.73) | data formatting | bytes 786432
